TPU v7x, 256 devices: a whole 4x4x8 slice. The times are simulated.
256 devices in a mesh: seq: 64 (over x, z, core), ch: 4 (over y).
Axes of the slice: x: 4, y: 4, z: 8, core: 2. Of those that a mesh axis runs over, the one named last changes fastest.
Arguments:
- proj: bfloat16 [3, 128, 65536], P(None, 'ch', 'seq'), may hold values from -6 to 6
- cotangent: bfloat16 [128, 65536], P('ch', 'seq'), may hold values from -6 to 6
- short_w: float32 [3, 128, 3], P(None, 'ch'), may hold values from -3.5 to 3.5
- filter_in: float32 [32, 64], replicated, may hold values from -5 to 5
- filter_out: float32 [64, 128], P(None, 'ch'), may hold values from -0.75 to 0.75
- rates: float32 [128], P('ch'), may hold values from 0.25 to 2184
Outputs:
- grad_proj: bfloat16 [3, 128, 65536], P(None, 'ch', 'seq')
- grad_short: float32 [3, 128, 3], P(None, 'ch')
- grad_filter_out: float32 [64, 128], P(None, 'ch')
- grad_filter_in: float32 [32, 64], replicated
All inputs are finite; a program needn't handle non-finite values.
Results may differ from a plain program's by a relative error of at most 0.0013.
Values may be sent and summed in bfloat16 or wider, within the bound.
A program may use at most 64 MiB of HBM per device.

v0:
```python
import math
import jax
import jax.numpy as jnp
from jax import lax
from jax.sharding import PartitionSpec as P

PRECISE = lax.Precision.HIGHEST


def shifted(value, axis, by):
    length = lax.axis_size(axis)
    pairs = [(i, i + by) for i in range(length) if 0 <= i + by < length]
    return lax.ppermute(value, axis, pairs)


def position_features(positions, length, feature_count):
    feature_index = jnp.arange(feature_count, dtype=jnp.int32)
    multiplier = (1 + feature_index // 2 * 499) % length
    upper = positions // 1024
    lower = positions % 1024
    phases = (
        upper[:, None] * (multiplier * 1024 % length)[None, :]
        + lower[:, None] * multiplier[None, :]
    ) % length
    angles = phases.astype(jnp.float32) * (2.0 * math.pi / length)
    return jnp.where((feature_index % 2 == 0)[None, :], jnp.cos(angles), jnp.sin(angles))


def angle_tables(row_count, col_count, row_start, col_start, modulus):
    row_index = row_start + jnp.arange(row_count, dtype=jnp.int32)
    col_index = col_start + jnp.arange(col_count, dtype=jnp.int32)
    phases = row_index[:, None] * col_index[None, :] % modulus
    angles = phases.astype(jnp.float32) * (2.0 * math.pi / modulus)
    return (jnp.cos(angles), jnp.sin(angles))


def rotate(real_part, imag_part, cosine, sine, sign):
    return (
        real_part * cosine - sign * imag_part * sine,
        imag_part * cosine + sign * real_part * sine,
    )


def dft_axis(real_part, imag_part, form, cosine, sine, sign):
    real_cos = jnp.einsum(form, real_part, cosine, precision=PRECISE)
    real_sin = jnp.einsum(form, real_part, sine, precision=PRECISE)
    imag_cos = jnp.einsum(form, imag_part, cosine, precision=PRECISE)
    imag_sin = jnp.einsum(form, imag_part, sine, precision=PRECISE)
    return (real_cos - sign * imag_sin, imag_cos + sign * real_sin)


def shards(proj, cotangent, short_w, filter_in, filter_out, rates):
    tap_count = short_w.shape[2]
    channels = proj.shape[1]
    devices = lax.axis_size("seq")
    tokens_here = proj.shape[2]
    length = devices * tokens_here
    modulus = 2 * length
    norm_scale = 1.0 / math.sqrt(length)
    column_width = tokens_here // devices
    first_split = math.gcd(tokens_here, 64)
    second_split = tokens_here // first_split
    device_index = lax.axis_index("seq")
    rim_cols = shifted(proj[:, :, tokens_here - (tap_count - 1) :], "seq", 1)
    extended = jnp.concatenate([rim_cols, proj], 2).astype(jnp.float32)

    def delayed(offset):
        return extended[:, :, tap_count - 1 - offset : tap_count - 1 - offset + tokens_here]

    mixed_all = short_w[:, :, 0, None] * delayed(0)
    for offset in range(1, tap_count):
        mixed_all = mixed_all + short_w[:, :, offset, None] * delayed(offset)
    query_part, key_part, value_part = (mixed_all[0], mixed_all[1], mixed_all[2])
    gated_prod = key_part * value_part
    cotangent_full = cotangent.astype(jnp.float32)
    grad_conv = cotangent_full * query_part
    both_signals = jnp.concatenate([gated_prod, grad_conv], 0).reshape(2 * channels, 1, tokens_here)
    columns = lax.all_to_all(both_signals, "seq", split_axis=2, concat_axis=1, tiled=True)
    block_start = jnp.arange(devices, dtype=jnp.int32) * tokens_here
    offset_start = device_index * column_width + jnp.arange(column_width, dtype=jnp.int32)
    column_pos = (block_start[:, None] + offset_start[None, :]).reshape(devices * column_width)
    features = position_features(column_pos, length, filter_in.shape[0])
    preact = jnp.dot(features, filter_in, precision=PRECISE, preferred_element_type=jnp.float32)
    hidden = jnp.sin(preact)
    modulated = jnp.einsum("to,oc->ct", hidden, filter_out, precision=PRECISE)
    relative = column_pos.astype(jnp.float32) / length
    spread = jnp.sqrt(jnp.expm1(-2.0 * rates) / jnp.expm1(-2.0 * rates / length))
    envelope = jnp.exp(-rates[:, None] * relative[None, :]) / spread[:, None]
    kernel = (envelope * modulated).reshape(channels, devices, column_width)
    stacked = jnp.concatenate([columns[:channels], kernel, columns[channels:]], 0)
    cos_outer, sin_outer = angle_tables(devices, 2 * devices, 0, 0, 2 * devices)
    turned_real = jnp.einsum("ran,ak->rkn", stacked, cos_outer, precision=PRECISE)
    turned_imag = -jnp.einsum("ran,ak->rkn", stacked, sin_outer, precision=PRECISE)
    cos_turn, sin_turn = angle_tables(
        2 * devices, column_width, 0, device_index * column_width, modulus
    )
    turned_real, turned_imag = rotate(turned_real, turned_imag, cos_turn, sin_turn, -1.0)
    moved_real, moved_imag = (
        lax.all_to_all(turned_real, "seq", split_axis=1, concat_axis=2, tiled=True),
        lax.all_to_all(turned_imag, "seq", split_axis=1, concat_axis=2, tiled=True),
    )
    row_total = moved_real.shape[0]
    cos_first, sin_first = angle_tables(first_split, first_split, 0, 0, first_split)
    cos_second, sin_second = angle_tables(second_split, second_split, 0, 0, second_split)
    cos_mid, sin_mid = angle_tables(first_split, second_split, 0, 0, tokens_here)
    grid_real = moved_real.reshape(row_total, 2, first_split, second_split)
    grid_imag = moved_imag.reshape(row_total, 2, first_split, second_split)
    grid_real, grid_imag = dft_axis(
        grid_real, grid_imag, "rkab,ac->rkcb", cos_first, sin_first, -1.0
    )
    grid_real, grid_imag = rotate(grid_real, grid_imag, cos_mid, sin_mid, -1.0)
    spec_real, spec_imag = dft_axis(
        grid_real, grid_imag, "rkcb,bd->rkcd", cos_second, sin_second, -1.0
    )
    gated_real, gated_imag = (spec_real[:channels], spec_imag[:channels])
    kernel_real, kernel_imag = (
        spec_real[channels : 2 * channels],
        spec_imag[channels : 2 * channels],
    )
    grad_real, grad_imag = (spec_real[2 * channels :], spec_imag[2 * channels :])
    conv_real = gated_real * kernel_real - gated_imag * kernel_imag
    conv_imag = gated_real * kernel_imag + gated_imag * kernel_real
    back_real = grad_real * kernel_real + grad_imag * kernel_imag
    back_imag = grad_imag * kernel_real - grad_real * kernel_imag
    kgrad_real = grad_real * gated_real + grad_imag * gated_imag
    kgrad_imag = grad_imag * gated_real - grad_real * gated_imag
    cos_back, sin_back = angle_tables(2, tokens_here, 2 * device_index, 0, modulus)
    cos_last, sin_last = angle_tables(2 * devices, devices, 0, 0, 2 * devices)
    real_part = jnp.concatenate([conv_real, back_real, kgrad_real], 0)
    rows = real_part.shape[0]
    part_real, part_imag = dft_axis(
        real_part,
        jnp.concatenate([conv_imag, back_imag, kgrad_imag], 0),
        "rkcd,db->rkcb",
        cos_second,
        sin_second,
        1.0,
    )
    part_real, part_imag = rotate(part_real, part_imag, cos_mid, sin_mid, 1.0)
    part_real, part_imag = dft_axis(
        part_real, part_imag, "rkcb,ca->rkab", cos_first, sin_first, 1.0
    )
    part_real = part_real.reshape(rows, 2, tokens_here)
    part_imag = part_imag.reshape(rows, 2, tokens_here)
    part_real, part_imag = rotate(part_real, part_imag, cos_back[None], sin_back[None], 1.0)
    spread_real = lax.all_to_all(part_real, "seq", split_axis=2, concat_axis=1, tiled=True)
    spread_imag = lax.all_to_all(part_imag, "seq", split_axis=2, concat_axis=1, tiled=True)
    real_out = jnp.einsum("rkn,ka->ran", spread_real, cos_last, precision=PRECISE)
    real_out = (real_out - jnp.einsum("rkn,ka->ran", spread_imag, sin_last, precision=PRECISE)) * (
        1.0 / modulus
    )
    conv_cols = real_out[:channels]
    gated_cols = real_out[channels : 2 * channels]
    kernel_grad = real_out[2 * channels :]
    returned = lax.all_to_all(
        jnp.concatenate([conv_cols, gated_cols], 0), "seq", split_axis=1, concat_axis=2, tiled=True
    )
    returned = returned.reshape(2 * channels, tokens_here)
    conv_out = returned[:channels]
    grad_gated = returned[channels:]
    grad_mixed = jnp.stack(
        [cotangent_full * conv_out, grad_gated * value_part, grad_gated * key_part]
    )
    short_part = jnp.stack(
        [jnp.sum(grad_mixed * delayed(offset), axis=2) for offset in range(tap_count)], axis=2
    )
    weighted = envelope * kernel_grad.reshape(channels, devices * column_width)
    out_part = jnp.einsum("to,ct->oc", hidden, weighted, precision=PRECISE)
    grad_hidden = jnp.einsum("ct,oc->to", weighted, filter_out, precision=PRECISE)
    in_part = jnp.einsum("tf,to->fo", features, grad_hidden * jnp.cos(preact), precision=PRECISE)
    next_rim = shifted(grad_mixed[:, :, : tap_count - 1], "seq", -1)
    grad_extended = jnp.concatenate([grad_mixed, next_rim], 2)
    result = short_w[:, :, 0, None] * grad_extended[:, :, 0:tokens_here]
    for offset in range(1, tap_count):
        result = (
            result
            + short_w[:, :, offset, None] * grad_extended[:, :, offset : offset + tokens_here]
        )
    grad_proj = result.astype(jnp.bfloat16)
    short_total, out_total = lax.psum((short_part, out_part), "seq")
    in_total = lax.psum(in_part, ("seq", "ch"))
    return (grad_proj, short_total * norm_scale, out_total * norm_scale, in_total * norm_scale)


def solution(mesh):
    placed = (
        P(None, "ch", "seq"),
        P("ch", "seq"),
        P(None, "ch", None),
        P(),
        P(None, "ch"),
        P("ch"),
    )
    return jax.shard_map(
        shards,
        mesh=mesh,
        in_specs=placed,
        out_specs=(P(None, "ch", "seq"), P(None, "ch", None), P(None, "ch"), P()),
        check_vma=False,
    )
```

profile of v0, /device:TPU:8, one launch (start us, length us, event | category | flops | bytes accessed | tf_op | source)
XLA Modules:
  0.0 598.5 jit_solution(10087766709720511439)
XLA Ops:
  4.3 5.1 fusion.244
  12.4 3.8 reduce
  16.2 2.1 reshape.320
  18.3 13.3 %all-to-all-start = ((f32[64,1,1024]{2,1,0:T(1,128)}), f32[64,1,1024]{2,1,0:T(1,128)}, u32[]{:S(2)}, u32[]{:S(2)}) async-start(f32[64,1,1024]{2,1,0:T(1,128)} %reshape.320), calls=%async_computation | async-start | bytes 524288 | tf_op jit(solution)/shard_map/all_to_all | solution.py:78
  37.6 5.8 all-to-all-done
  43.4 2.9 reduce.1
  46.4 2.4 reshape.321
  48.8 2.3 fusion.241
  53.9 2.9 add_bitcast_fusion.1
  56.9 2.5 copy.152
  59.4 6.3 %all-to-all-start.2 = ((f32[96,128,16]{0,2,1:T(8,128)}), f32[96,128,16]{0,2,1:T(8,128)}, u32[]{:S(2)}, u32[]{:S(2)}) async-start(f32[96,128,16]{0,2,1:T(8,128)} %copy.152), calls=%async_computation.2 | async-start | bytes 2097152 | tf_op jit(solution)/shard_map/all_to_all | solution.py:100
  65.6 2.5 copy.150
  68.2 25.5 %all-to-all-done.2 = f32[96,128,16]{0,2,1:T(8,128)} async-done(((f32[96,128,16]{0,2,1:T(8,128)}), f32[96,128,16]{0,2,1:T(8,128)}, u32[]{:S(2)}, u32[]{:S(2)}) %all-to-all-start.2) | async-done | bytes 786464 | tf_op jit(solution)/shard_map/all_to_all | solution.py:100
  93.7 7.2 %all-to-all-start.1 = ((f32[96,128,16]{0,2,1:T(8,128)}), f32[96,128,16]{0,2,1:T(8,128)}, u32[]{:S(2)}, u32[]{:S(2)}) async-start(f32[96,128,16]{0,2,1:T(8,128)} %copy.150), calls=%async_computation.1 | async-start | bytes 2097152 | tf_op jit(solution)/shard_map/all_to_all | solution.py:99
  101.4 3.8 fusion.14
  105.3 23.3 %all-to-all-done.1 = f32[96,128,16]{0,2,1:T(8,128)} async-done(((f32[96,128,16]{0,2,1:T(8,128)}), f32[96,128,16]{0,2,1:T(8,128)}, u32[]{:S(2)}, u32[]{:S(2)}) %all-to-all-start.1) | async-done | bytes 786464 | tf_op jit(solution)/shard_map/all_to_all | solution.py:99
  128.5 2.9 fusion.18
  131.5 2.9 fusion.7
  134.4 3.4 subtract_bitcast_fusion
  163.5 6.8 %all-to-all-start.3 = ((f32[96,2,1024]{0,1,2:T(2,128)}), f32[96,2,1024]{0,1,2:T(2,128)}, u32[]{:S(2)}, u32[]{:S(2)}) async-start(f32[96,2,1024]{0,1,2:T(2,128)} %copy.166), calls=%async_computation.3 | async-start | bytes 2097152 | tf_op jit(solution)/shard_map/all_to_all | solution.py:146
  170.4 3.0 copy.170
  173.4 25.0 %all-to-all-done.3 = f32[96,2,1024]{0,1,2:T(2,128)} async-done(((f32[96,2,1024]{0,1,2:T(2,128)}), f32[96,2,1024]{0,1,2:T(2,128)}, u32[]{:S(2)}, u32[]{:S(2)}) %all-to-all-start.3) | async-done | bytes 786464 | tf_op jit(solution)/shard_map/all_to_all | solution.py:146
  198.4 6.8 %all-to-all-start.4 = ((f32[96,2,1024]{0,1,2:T(2,128)}), f32[96,2,1024]{0,1,2:T(2,128)}, u32[]{:S(2)}, u32[]{:S(2)}) async-start(f32[96,2,1024]{0,1,2:T(2,128)} %copy.170), calls=%async_computation.4 | async-start | bytes 2097152 | tf_op jit(solution)/shard_map/all_to_all | solution.py:147
  208.5 24.7 %all-to-all-done.4 = f32[96,2,1024]{0,1,2:T(2,128)} async-done(((f32[96,2,1024]{0,1,2:T(2,128)}), f32[96,2,1024]{0,1,2:T(2,128)}, u32[]{:S(2)}, u32[]{:S(2)}) %all-to-all-start.4) | async-done | bytes 786464 | tf_op jit(solution)/shard_map/all_to_all | solution.py:147
  238.8 2.1 reshape.322
  240.9 7.0 %all-to-all-start.5 = ((f32[64,1,1024]{2,1,0:T(1,128)}), f32[64,1,1024]{2,1,0:T(1,128)}, u32[]{:S(2)}, u32[]{:S(2)}) async-start(f32[64,1,1024]{2,1,0:T(1,128)} %reshape.322), calls=%async_computation.5 | async-start | bytes 524288 | tf_op jit(solution)/shard_map/all_to_all | solution.py:155
  247.8 2.2 copy.175
  251.9 2.2 convolution_multiply_fusion.4
  254.1 3.0 fusion.43
  257.1 75.9 %psum.23 = f32[32,64]{1,0:T(8,128)S(1)} all-reduce(f32[32,64]{1,0:T(8,128)S(1)} %fusion.43), channel_id=1, replica_groups=mesh['seq'=64,'ch'=4] {'seq','ch'}, use_global_device_ids=true, to_apply=%region_5.6 | all-reduce | flops 2048 | bytes 16384 | tf_op jit(solution)/shard_map/psum | solution.py:181
  334.4 2.9 reduce.2
  346.4 250.5 %all-reduce = (f32[3,32,3]{1,0,2:T(4,128)S(1)}, f32[64,32]{0,1:T(8,128)S(1)}) all-reduce(f32[3,32,3]{1,0,2:T(4,128)S(1)} %pad_maximum_fusion.7, f32[64,32]{0,1:T(8,128)S(1)} %fusion.238), channel_id=1, replica_groups=mesh['seq'=64,'ch'=4] {'seq'}, use_global_device_ids=true, to_apply=%region_3.4 | all-reduce | flops 2336 | bytes 18688 | tf_op jit(solution)/shard_map/psum | solution.py:180
  (110 shorter events, 63.7 us)
Async XLA Ops:
  0.6 3.7 copy-start
  0.6 8.8 %copy-start.6 = (bf16[32,1024]{1,0:T(8,128)(2,1)S(1)}, bf16[32,1024]{1,0:T(8,128)(2,1)}, u32[]{:S(2)}) copy-start(bf16[32,1024]{1,0:T(8,128)(2,1)} %param.7) | copy-start | bytes 196612
  1.5 8.1 %collective-permute-start = (bf16[3,32,2]{2,1,0:T(8,128)(2,1)S(1)}, bf16[3,32,2]{2,1,0:T(8,128)(2,1)S(1)}, u32[]{:S(2)}, u32[]{:S(2)}) collective-permute-start(bf16[3,32,2]{2,1,0:T(8,128)(2,1)S(1)} %slice.96), channel_id=1, source_target_pairs={{0,4},{4,8},{8,12},{12,16},{16,20},{20,24},{24,28},{28,32},{32,36}... | collective-permute-start | bytes 1160 | tf_op jit(solution)/shard_map/ppermute | solution.py:13
  3.3 6.3 %copy-start.10 = (s32[32]{0:T(128)}, s32[32]{0:T(128)S(1)}, u32[]{:S(2)}) copy-start(s32[32]{0:T(128)S(1)} %get-tuple-element.66) | copy-start | bytes 388
  3.3 6.3 %copy-start.12 = (pred[32]{0:T(512)(128)(4,1)}, pred[32]{0:T(512)(128)(4,1)S(1)}, u32[]{:S(2)}) copy-start(pred[32]{0:T(512)(128)(4,1)S(1)} %fusion.143) | copy-start | bytes 100
  4.3 5.3 copy-start.5
  11.9 19.7 %copy-start.9 = (f32[32]{0:T(128)S(1)}, f32[32]{0:T(128)}, u32[]{:S(2)}) copy-start(f32[32]{0:T(128)} %param.11) | copy-start | bytes 388
  11.9 19.7 %copy-start.7 = (f32[64,32]{0,1:T(8,128)S(1)}, f32[64,32]{0,1:T(8,128)}, u32[]{:S(2)}) copy-start(f32[64,32]{0,1:T(8,128)} %param.10) | copy-start | bytes 24580
  18.3 25.2 %all-to-all-start = ((f32[64,1,1024]{2,1,0:T(1,128)}), f32[64,1,1024]{2,1,0:T(1,128)}, u32[]{:S(2)}, u32[]{:S(2)}) async-start(f32[64,1,1024]{2,1,0:T(1,128)} %reshape.320), calls=%async_computation | async-start | bytes 524288 | tf_op jit(solution)/shard_map/all_to_all | solution.py:78
  51.1 1.0 copy-start.2
  59.4 34.3 %all-to-all-start.2 = ((f32[96,128,16]{0,2,1:T(8,128)}), f32[96,128,16]{0,2,1:T(8,128)}, u32[]{:S(2)}, u32[]{:S(2)}) async-start(f32[96,128,16]{0,2,1:T(8,128)} %copy.152), calls=%async_computation.2 | async-start | bytes 2097152 | tf_op jit(solution)/shard_map/all_to_all | solution.py:100
  93.7 34.9 %all-to-all-start.1 = ((f32[96,128,16]{0,2,1:T(8,128)}), f32[96,128,16]{0,2,1:T(8,128)}, u32[]{:S(2)}, u32[]{:S(2)}) async-start(f32[96,128,16]{0,2,1:T(8,128)} %copy.150), calls=%async_computation.1 | async-start | bytes 2097152 | tf_op jit(solution)/shard_map/all_to_all | solution.py:99
  128.5 3.0 copy-start.3
  163.5 34.9 %all-to-all-start.3 = ((f32[96,2,1024]{0,1,2:T(2,128)}), f32[96,2,1024]{0,1,2:T(2,128)}, u32[]{:S(2)}, u32[]{:S(2)}) async-start(f32[96,2,1024]{0,1,2:T(2,128)} %copy.166), calls=%async_computation.3 | async-start | bytes 2097152 | tf_op jit(solution)/shard_map/all_to_all | solution.py:146
  198.4 34.9 %all-to-all-start.4 = ((f32[96,2,1024]{0,1,2:T(2,128)}), f32[96,2,1024]{0,1,2:T(2,128)}, u32[]{:S(2)}, u32[]{:S(2)}) async-start(f32[96,2,1024]{0,1,2:T(2,128)} %copy.170), calls=%async_computation.4 | async-start | bytes 2097152 | tf_op jit(solution)/shard_map/all_to_all | solution.py:147
  234.5 1.0 copy-start.4
  238.8 13.1 %copy-start.8 = (f32[64,32]{0,1:T(8,128)S(1)}, f32[64,32]{0,1:T(8,128)}, u32[]{:S(2)}) copy-start(f32[64,32]{0,1:T(8,128)} %param.10) | copy-start | bytes 24580
  240.9 13.2 %copy-start.11 = (s32[32]{0:T(128)S(1)}, s32[32]{0:T(128)}, u32[]{:S(2)}) copy-start(s32[32]{0:T(128)} %copy-done.10) | copy-start | bytes 388
  240.9 13.2 %copy-start.13 = (pred[32]{0:T(512)(128)(4,1)S(1)}, pred[32]{0:T(512)(128)(4,1)}, u32[]{:S(2)}) copy-start(pred[32]{0:T(512)(128)(4,1)} %copy-done.12) | copy-start | bytes 100
  240.9 93.6 %all-to-all-start.5 = ((f32[64,1,1024]{2,1,0:T(1,128)}), f32[64,1,1024]{2,1,0:T(1,128)}, u32[]{:S(2)}, u32[]{:S(2)}) async-start(f32[64,1,1024]{2,1,0:T(1,128)} %reshape.322), calls=%async_computation.5 | async-start | bytes 524288 | tf_op jit(solution)/shard_map/all_to_all | solution.py:155
  341.0 3.1 collective-permute-start.1
  344.1 253.9 %copy-start.1 = (f32[32,64]{1,0:T(8,128)S(1)}, f32[32,64]{1,0:T(8,128)}, u32[]{:S(2)}) copy-start(f32[32,64]{1,0:T(8,128)} %param.9) | copy-start | bytes 24580
where the time goes:
time: 605 us; the launch traced here: 599 us
  blocking collectives  326 us (54%)
  waiting for transfers between devices  106 us (18%)
  matrix products  52.9 us (9%)
  starting transfers between devices  50.4 us (8%)
  local copies, waits for them, and re-layouts  42.8 us (7%)
  other arithmetic  18.9 us (3%)
    psum x1, blocking collectives, shards(): short_total, out_total = lax.psum((short_part, out_part), 'seq')  250 us
    psum x1, blocking collectives, shards(): in_total = lax.psum(in_part, ('seq', 'ch'))  75.9 us
    all_to_all x1, waiting for transfers between devices, shards(): lax.all_to_all(turned_imag, 'seq', split_axis=1, concat_axis=2, tiled=True)  25.5 us
    all_to_all x1, waiting for transfers between devices, shards(): lax.all_to_all(part_real, 'seq', split_axis=2, concat_axis=1, tiled=True)  25 us
    all_to_all x1, waiting for transfers between devices, shards(): lax.all_to_all(part_imag, 'seq', split_axis=2, concat_axis=1, tiled=True)  24.7 us
    all_to_all x1, waiting for transfers between devices, shards(): lax.all_to_all(turned_real, 'seq', split_axis=1, concat_axis=2, tiled=True)  23.3 us
    all_to_all x1, starting transfers between devices, shards(): lax.all_to_all(both_signals, 'seq', split_axis=2, concat_axis=1, tiled=True)  13.3 us
    unnamed x38, local copies, waits for them, and re-layouts  12.3 us
  transfers between devices with their start and end apart: 8, of which 6 were waited for; matrix products, arithmetic and copies ran while one was open for 6% of the time, Pallas kernels for 0%

commit v1 on v0

--- a/solution.py
+++ b/solution.py
@@ -3,6 +3,7 @@
 import jax.numpy as jnp
 from jax import lax
 from jax.sharding import PartitionSpec as P
+from jax.lax import all_gather
 
 PRECISE = lax.Precision.HIGHEST
 
@@ -178,7 +179,7 @@
         )
     grad_proj = result.astype(jnp.bfloat16)
     short_total, out_total = lax.psum((short_part, out_part), "seq")
-    in_total = lax.psum(in_part, ("seq", "ch"))
+    in_total = jnp.sum(all_gather(in_part, ("seq", "ch")), axis=0)
     return (grad_proj, short_total * norm_scale, out_total * norm_scale, in_total * norm_scale)
 
 

time: 605 us -> 555 us (0.917)
  blocking collectives: 326 us -> 268 us
  between operations: 1.66 us -> 15.1 us
  starting transfers between devices: 50.4 us -> 43.8 us
    psum x1 -> x0, blocking collectives: 75.9 us -> none  [shards(): in_total = lax.psum(in_part, ('seq', 'ch'))]
    all_to_all x0 -> x1, blocking collectives: none -> 18.8 us  [shards(): lax.all_to_all(jnp.concatenate([conv_cols, gated_cols], 0), 'seq', split_...]
    all_to_all x1 -> x0, starting transfers between devices: 6.96 us -> none  [shards(): lax.all_to_all(jnp.concatenate([conv_cols, gated_cols], 0), 'seq', split_...]
    unnamed x38 -> x44, local copies, waits for them, and re-layouts: 12.3 us -> 13.2 us
  transfers between devices with their start and end apart: 8 -> 8, of which waited for: 6 -> 6; matrix products, arithmetic and copies ran while one was open for 6% -> 7% of each run, Pallas kernels for 0% -> 0%
where the time goes in v1:
time: 555 us; the launch traced here: 548 us
  blocking collectives  268 us (48%)
  waiting for transfers between devices  105 us (19%)
  matrix products  52.4 us (9%)
  starting transfers between devices  43.8 us (8%)
  local copies, waits for them, and re-layouts  42.8 us (8%)
  other arithmetic  21.5 us (4%)
  between operations  15.1 us (3%)
    psum x1, blocking collectives, shards(): short_total, out_total = lax.psum((short_part, out_part), 'seq')  249 us
    all_to_all x1, waiting for transfers between devices, shards(): lax.all_to_all(turned_imag, 'seq', split_axis=1, concat_axis=2, tiled=True)  25.5 us
    all_to_all x1, waiting for transfers between devices, shards(): lax.all_to_all(part_real, 'seq', split_axis=2, concat_axis=1, tiled=True)  25 us
    all_to_all x1, waiting for transfers between devices, shards(): lax.all_to_all(part_imag, 'seq', split_axis=2, concat_axis=1, tiled=True)  24.4 us
    all_to_all x1, waiting for transfers between devices, shards(): lax.all_to_all(turned_real, 'seq', split_axis=1, concat_axis=2, tiled=True)  23.3 us
    all_to_all x1, blocking collectives, shards(): lax.all_to_all(jnp.concatenate([conv_cols, gated_cols], 0), 'seq', split_...  18.8 us
    all_to_all x1, starting transfers between devices, shards(): lax.all_to_all(both_signals, 'seq', split_axis=2, concat_axis=1, tiled=True)  13.3 us
    unnamed x44, local copies, waits for them, and re-layouts  13.2 us
  transfers between devices with their start and end apart: 8, of which 6 were waited for; matrix products, arithmetic and copies ran while one was open for 7% of the time, Pallas kernels for 0%

profile of v1, /device:TPU:8, one launch (start us, length us, event | category | flops | bytes accessed | tf_op | source)
XLA Modules:
  0.0 548.4 jit_solution(8592697006358385771)
XLA Ops:
  10.9 5.1 fusion.244
  19.0 3.8 reduce
  22.8 2.1 reshape.321
  24.9 13.3 %all-to-all-start = ((f32[64,1,1024]{2,1,0:T(1,128)}), f32[64,1,1024]{2,1,0:T(1,128)}, u32[]{:S(2)}, u32[]{:S(2)}) async-start(f32[64,1,1024]{2,1,0:T(1,128)} %reshape.321), calls=%async_computation | async-start | bytes 524288 | tf_op jit(solution)/shard_map/all_to_all | solution.py:79
  44.2 5.8 %all-to-all-done = f32[64,1,1024]{2,1,0:T(1,128)} async-done(((f32[64,1,1024]{2,1,0:T(1,128)}), f32[64,1,1024]{2,1,0:T(1,128)}, u32[]{:S(2)}, u32[]{:S(2)}) %all-to-all-start) | async-done | bytes 262176 | tf_op jit(solution)/shard_map/all_to_all | solution.py:79
  50.0 2.9 reduce.1
  53.0 2.5 reshape.322
  55.4 2.3 fusion.241
  60.6 2.9 add_bitcast_fusion.1
  63.4 2.5 copy.152
  65.9 6.3 %all-to-all-start.2 = ((f32[96,128,16]{0,2,1:T(8,128)}), f32[96,128,16]{0,2,1:T(8,128)}, u32[]{:S(2)}, u32[]{:S(2)}) async-start(f32[96,128,16]{0,2,1:T(8,128)} %copy.152), calls=%async_computation.2 | async-start | bytes 2097152 | tf_op jit(solution)/shard_map/all_to_all | solution.py:101
  72.2 2.5 copy.150
  74.7 25.5 %all-to-all-done.2 = f32[96,128,16]{0,2,1:T(8,128)} async-done(((f32[96,128,16]{0,2,1:T(8,128)}), f32[96,128,16]{0,2,1:T(8,128)}, u32[]{:S(2)}, u32[]{:S(2)}) %all-to-all-start.2) | async-done | bytes 786464 | tf_op jit(solution)/shard_map/all_to_all | solution.py:101
  100.2 7.2 %all-to-all-start.1 = ((f32[96,128,16]{0,2,1:T(8,128)}), f32[96,128,16]{0,2,1:T(8,128)}, u32[]{:S(2)}, u32[]{:S(2)}) async-start(f32[96,128,16]{0,2,1:T(8,128)} %copy.150), calls=%async_computation.1 | async-start | bytes 2097152 | tf_op jit(solution)/shard_map/all_to_all | solution.py:100
  108.0 3.8 fusion.14
  111.8 23.3 %all-to-all-done.1 = f32[96,128,16]{0,2,1:T(8,128)} async-done(((f32[96,128,16]{0,2,1:T(8,128)}), f32[96,128,16]{0,2,1:T(8,128)}, u32[]{:S(2)}, u32[]{:S(2)}) %all-to-all-start.1) | async-done | bytes 786464 | tf_op jit(solution)/shard_map/all_to_all | solution.py:100
  135.1 2.9 fusion.18
  138.0 2.9 fusion.7
  140.9 3.4 subtract_bitcast_fusion
  170.0 6.8 %all-to-all-start.3 = ((f32[96,2,1024]{0,1,2:T(2,128)}), f32[96,2,1024]{0,1,2:T(2,128)}, u32[]{:S(2)}, u32[]{:S(2)}) async-start(f32[96,2,1024]{0,1,2:T(2,128)} %copy.166), calls=%async_computation.3 | async-start | bytes 2097152 | tf_op jit(solution)/shard_map/all_to_all | solution.py:147
  176.8 3.0 copy.170
  179.9 25.0 %all-to-all-done.3 = f32[96,2,1024]{0,1,2:T(2,128)} async-done(((f32[96,2,1024]{0,1,2:T(2,128)}), f32[96,2,1024]{0,1,2:T(2,128)}, u32[]{:S(2)}, u32[]{:S(2)}) %all-to-all-start.3) | async-done | bytes 786464 | tf_op jit(solution)/shard_map/all_to_all | solution.py:147
  204.9 6.8 %all-to-all-start.4 = ((f32[96,2,1024]{0,1,2:T(2,128)}), f32[96,2,1024]{0,1,2:T(2,128)}, u32[]{:S(2)}, u32[]{:S(2)}) async-start(f32[96,2,1024]{0,1,2:T(2,128)} %copy.170), calls=%async_computation.4 | async-start | bytes 2097152 | tf_op jit(solution)/shard_map/all_to_all | solution.py:148
  215.3 24.4 %all-to-all-done.4 = f32[96,2,1024]{0,1,2:T(2,128)} async-done(((f32[96,2,1024]{0,1,2:T(2,128)}), f32[96,2,1024]{0,1,2:T(2,128)}, u32[]{:S(2)}, u32[]{:S(2)}) %all-to-all-start.4) | async-done | bytes 786464 | tf_op jit(solution)/shard_map/all_to_all | solution.py:148
  247.1 2.2 convolution_multiply_fusion.4
  249.4 3.6 fusion.43
  253.1 2.1 copy.229
  255.2 2.1 reshape.323
  257.3 18.8 %all_to_all.84 = f32[64,1,1024]{2,1,0:T(1,128)} all-to-all(f32[64,1,1024]{2,1,0:T(1,128)} %reshape.323), channel_id=1, replica_groups=mesh['seq'=64,'ch'=4] {'seq'}, dimensions={0} | all-to-all | bytes 524288 | tf_op jit(solution)/shard_map/all_to_all | solution.py:156
  276.0 2.9 reduce.2
  288.0 248.8 %all-reduce = (f32[3,32,3]{1,0,2:T(4,128)S(1)}, f32[64,32]{0,1:T(8,128)S(1)}) all-reduce(f32[3,32,3]{1,0,2:T(4,128)S(1)} %pad_maximum_fusion.7, f32[64,32]{0,1:T(8,128)S(1)} %fusion.238), channel_id=1, replica_groups=mesh['seq'=64,'ch'=4] {'seq'}, use_global_device_ids=true, to_apply=%region_3.4 | all-reduce | flops 2336 | bytes 18688 | tf_op jit(solution)/shard_map/psum | solution.py:181
  538.0 2.5 reduce_sum.39
  (118 shorter events, 63.2 us)
Async XLA Ops:
  7.2 3.7 copy-start
  7.2 8.8 %copy-start.8 = (bf16[32,1024]{1,0:T(8,128)(2,1)S(1)}, bf16[32,1024]{1,0:T(8,128)(2,1)}, u32[]{:S(2)}) copy-start(bf16[32,1024]{1,0:T(8,128)(2,1)} %param.7) | copy-start | bytes 196612
  8.0 8.1 %collective-permute-start = (bf16[3,32,2]{2,1,0:T(8,128)(2,1)S(1)}, bf16[3,32,2]{2,1,0:T(8,128)(2,1)S(1)}, u32[]{:S(2)}, u32[]{:S(2)}) collective-permute-start(bf16[3,32,2]{2,1,0:T(8,128)(2,1)S(1)} %slice.96), channel_id=1, source_target_pairs={{0,4},{4,8},{8,12},{12,16},{16,20},{20,24},{24,28},{28,32},{32,36}... | collective-permute-start | bytes 1160 | tf_op jit(solution)/shard_map/ppermute | solution.py:14
  9.8 6.3 %copy-start.12 = (s32[32]{0:T(128)}, s32[32]{0:T(128)S(1)}, u32[]{:S(2)}) copy-start(s32[32]{0:T(128)S(1)} %get-tuple-element.66) | copy-start | bytes 388
  9.8 6.3 %copy-start.14 = (pred[32]{0:T(512)(128)(4,1)}, pred[32]{0:T(512)(128)(4,1)S(1)}, u32[]{:S(2)}) copy-start(pred[32]{0:T(512)(128)(4,1)S(1)} %fusion.143) | copy-start | bytes 100
  10.9 5.3 copy-start.6
  18.5 19.7 %copy-start.11 = (f32[32]{0:T(128)S(1)}, f32[32]{0:T(128)}, u32[]{:S(2)}) copy-start(f32[32]{0:T(128)} %param.11) | copy-start | bytes 388
  18.5 19.7 %copy-start.9 = (f32[64,32]{0,1:T(8,128)S(1)}, f32[64,32]{0,1:T(8,128)}, u32[]{:S(2)}) copy-start(f32[64,32]{0,1:T(8,128)} %param.10) | copy-start | bytes 24580
  24.9 25.2 %all-to-all-start = ((f32[64,1,1024]{2,1,0:T(1,128)}), f32[64,1,1024]{2,1,0:T(1,128)}, u32[]{:S(2)}, u32[]{:S(2)}) async-start(f32[64,1,1024]{2,1,0:T(1,128)} %reshape.321), calls=%async_computation | async-start | bytes 524288 | tf_op jit(solution)/shard_map/all_to_all | solution.py:79
  57.8 1.0 copy-start.2
  65.9 34.3 %all-to-all-start.2 = ((f32[96,128,16]{0,2,1:T(8,128)}), f32[96,128,16]{0,2,1:T(8,128)}, u32[]{:S(2)}, u32[]{:S(2)}) async-start(f32[96,128,16]{0,2,1:T(8,128)} %copy.152), calls=%async_computation.2 | async-start | bytes 2097152 | tf_op jit(solution)/shard_map/all_to_all | solution.py:101
  100.2 34.9 %all-to-all-start.1 = ((f32[96,128,16]{0,2,1:T(8,128)}), f32[96,128,16]{0,2,1:T(8,128)}, u32[]{:S(2)}, u32[]{:S(2)}) async-start(f32[96,128,16]{0,2,1:T(8,128)} %copy.150), calls=%async_computation.1 | async-start | bytes 2097152 | tf_op jit(solution)/shard_map/all_to_all | solution.py:100
  135.1 2.9 copy-start.4
  170.0 34.9 %all-to-all-start.3 = ((f32[96,2,1024]{0,1,2:T(2,128)}), f32[96,2,1024]{0,1,2:T(2,128)}, u32[]{:S(2)}, u32[]{:S(2)}) async-start(f32[96,2,1024]{0,1,2:T(2,128)} %copy.166), calls=%async_computation.3 | async-start | bytes 2097152 | tf_op jit(solution)/shard_map/all_to_all | solution.py:147
  204.9 34.9 %all-to-all-start.4 = ((f32[96,2,1024]{0,1,2:T(2,128)}), f32[96,2,1024]{0,1,2:T(2,128)}, u32[]{:S(2)}, u32[]{:S(2)}) async-start(f32[96,2,1024]{0,1,2:T(2,128)} %copy.170), calls=%async_computation.4 | async-start | bytes 2097152 | tf_op jit(solution)/shard_map/all_to_all | solution.py:148
  211.7 326.3 %all-gather.3.cloned.1.call-start = ((), (), s32[]{:S(2)}) async-start(), calls=%async_computation.6 | async-start | bytes 4210688 | tf_op jit(solution)/shard_map/all_gather | solution.py:182
  241.0 1.0 copy-start.5
  243.1 0.8 copy-start.3
  243.9 3.2 copy-start.10
  243.9 5.4 copy-start.13
  243.9 5.4 copy-start.15
  282.5 1.4 copy-start.7
  282.5 1.4 copy-start.16
  282.6 3.1 collective-permute-start.1
  538.0 3.2 copy-start.1
Sparse Core Ops, SparseCore 0:
  253.2 112.9 all-gather.2
